TPU v7x, 256 devices: a whole 4x4x8 slice. The times are simulated.
256 devices in a mesh: cfg: 2 (over x_lo), wide: 32 (over x_hi, z, core), narrow: 4 (over y).
Axes of the slice: x: 4 (x_hi: 2, x_lo: 2; x = x_hi * 2 + x_lo), y: 4, z: 8, core: 2. Of those that a mesh axis runs over, the one named last changes fastest.
Arguments:
- hidden: bfloat16 [2, 4096, 3072], P('cfg', 'wide', 'narrow'), may hold values from -120 to 120
- split_table: int32 [32], replicated, may hold values from 1 to 128, 2048 in all
- modulation: float32 [8, 3072], P(None, 'narrow'), may hold values from -4 to 4
- expand_weight: bfloat16 [3072, 12288], P('narrow', 'wide'), may hold values from -0.109375 to 0.109375
- contract_weight: bfloat16 [12288, 3072], P('wide', 'narrow'), may hold values from -0.0546875 to 0.0546875
- output_weight: bfloat16 [3072, 64], P('narrow'), may hold values from -0.109375 to 0.109375
- latent: float32 [4096, 64], P('wide'), may hold values from -6 to 6
- timestep: int32 [1], replicated, may hold values from 20 to 499
Outputs:
- layer_out: bfloat16 [2, 4096, 3072], P('cfg', 'wide', 'narrow')
- clean_latent: float32 [4096, 64], P('wide')
Inputs may be any that keep to these rules, and one draw needn't show every extreme that they name: `split_table`: the entries sum to 2048, and the largest is exactly 128.
All inputs are finite; a program needn't handle non-finite values.
Results may differ from a plain program's by a relative error of at most 0.0056.
Values may be sent and summed in bfloat16 or wider, within the bound.
A program may use at most 64 MiB of HBM per device.

v0:
```python
import jax
import jax.numpy as jnp
from jax import lax
from jax.sharding import PartitionSpec as P

D = 3072
TEXT = 226
norm_eps = 1e-05
guidance = 6.0


def alpha_table():
    steps_index = jnp.arange(1000, dtype=jnp.int32)
    start_root = 0.00085**0.5
    end_root = 0.012**0.5
    roots = start_root + (end_root - start_root) * steps_index.astype(jnp.float32) / 999.0
    return (steps_index, jnp.cumprod(1.0 - roots * roots))


def feature_norm(values, shifts, scaling):
    totals, squares = lax.psum(
        (jnp.sum(values, -1, keepdims=True), jnp.sum(values * values, -1, keepdims=True)), "narrow"
    )
    average = totals / D
    variance = squares / D - average * average
    return (values - average) * lax.rsqrt(variance + norm_eps) * (1.0 + scaling) + shifts


def on_device(
    hidden, split_table, modulation, expand_weight, contract_weight, output_weight, latent, timestep
):
    capacity = hidden.shape[1]
    wide_index = lax.axis_index("wide")
    table_index = jnp.arange(split_table.shape[0], dtype=jnp.int32)
    offset = jnp.sum(jnp.where(table_index < wide_index, split_table, 0))
    own_count = jnp.sum(jnp.where(table_index == wide_index, split_table, 0))
    slot_index = jnp.arange(capacity, dtype=jnp.int32)
    position = offset + slot_index
    slot_live = slot_index < own_count
    is_text = slot_live & (position < TEXT)
    is_video = slot_live & (position >= TEXT)
    text_column = is_text[:, None]
    shifts = jnp.where(text_column, modulation[3], modulation[0])
    scaling = jnp.where(text_column, modulation[4], modulation[1])
    gating = jnp.where(text_column, modulation[5], modulation[2])
    values = hidden[0].astype(jnp.float32)
    normed = feature_norm(values, shifts, scaling).astype(jnp.bfloat16)
    hidden_part = jnp.dot(
        lax.all_gather(normed, "wide", axis=0, tiled=True),
        expand_weight,
        preferred_element_type=jnp.float32,
    )
    hidden_pre = lax.psum(hidden_part, "narrow")
    activated = jax.nn.gelu(hidden_pre, approximate=True).astype(jnp.bfloat16)
    ff_result = lax.psum_scatter(
        jnp.dot(activated, contract_weight, preferred_element_type=jnp.float32),
        "wide",
        scatter_dimension=0,
        tiled=True,
    )
    layer_out = jnp.where(slot_live[:, None], values + gating * ff_result, 0.0).astype(jnp.bfloat16)
    final_in = layer_out.astype(jnp.float32)
    final_normed = feature_norm(final_in, modulation[6], modulation[7]).astype(jnp.bfloat16)
    velocity_part = jnp.dot(final_normed, output_weight, preferred_element_type=jnp.float32)
    copy_weight = jnp.where(lax.axis_index("cfg") == 0, guidance, 1.0 - guidance)
    guided = lax.psum(velocity_part * copy_weight, ("cfg", "narrow"))
    steps_index, alpha_bar = alpha_table()
    alpha_now = jnp.sum(jnp.where(steps_index == timestep[0], alpha_bar, 0.0))
    clean_latent = jnp.where(
        is_video[:, None], jnp.sqrt(alpha_now) * latent - jnp.sqrt(1.0 - alpha_now) * guided, 0.0
    )
    return (layer_out[None], clean_latent)


def solution(mesh):
    return jax.shard_map(
        on_device,
        mesh=mesh,
        in_specs=(
            P("cfg", "wide", "narrow"),
            P(),
            P(None, "narrow"),
            P("narrow", "wide"),
            P("wide", "narrow"),
            P("narrow", None),
            P("wide", None),
            P(),
        ),
        out_specs=(P("cfg", "wide", "narrow"), P("wide", None)),
        check_vma=False,
    )
```

profile of v0, /device:TPU:2, one launch (start us, length us, event | category | flops | bytes accessed | tf_op | source)
XLA Modules:
  0.0 493.6 jit_solution(13559903819700724804)
XLA Ops:
  7.2 0.0 copy-start
  7.2 0.0 all-gather.2.cloned.1.call-start
  7.2 1.1 convert_reduce_fusion.1
  8.3 1.1 fusion.21
  9.4 1.1 add_reduce_fusion
  10.5 1.3 fusion.34
  11.8 1.3 compare_and_fusion.1
  13.1 10.7 %all-reduce.2 = (f32[128,1]{0,1:T(1,128)S(1)}, f32[128,1]{0,1:T(1,128)S(1)}) all-reduce(f32[128,1]{0,1:T(1,128)S(1)} %bitcast.48, f32[128,1]{0,1:T(1,128)S(1)} %bitcast.47), channel_id=1, replica_groups=mesh['cfg'=2,'wide'=32,'narrow'=4] {'narrow'}, use_global_device_ids=true, to_apply=%region_5.6 | all-reduce | flops 256 | bytes 2048 | tf_op jit(solution)/shard_map/psum | solution.py:21
  23.8 1.8 fusion.20
  25.7 0.0 all-gather.2.cloned.1.call-update
  25.7 0.0 all-reduce.5.cloned.1.call-start
  25.7 94.3 %all-gather.2.cloned.1.call-done = bf16[4096,768]{1,0:T(8,128)(2,1)} async-done(((bf16[128,768]{1,0:T(8,128)(2,1)}), bf16[4096,768]{1,0:T(8,128)(2,1)}) %all-gather.2.cloned.1.call-update) | async-done | bytes 6291472 | tf_op jit(solution)/shard_map/all_gather | solution.py:49
  120.1 9.0 %fusion.41 = f32[4096,384]{1,0:T(8,128)} fusion(bf16[4096,768]{1,0:T(8,128)(2,1)} %all-gather.2.cloned.1.call-done, bf16[768,384]{1,0:T(8,128)(2,1)} %param.11), kind=kOutput, calls=%fused_computation.70 | convolution fusion | flops 2415919104 | bytes 13172736 | tf_op jit(solution)/shard_map/dot_general | solution.py:48
  129.0 0.0 all-reduce.5.cloned.1.call-update
  129.1 0.0 reduce-scatter.2.cloned.1.call-start
  129.1 129.7 %all-reduce.5.cloned.1.call-done = f32[4096,384]{1,0:T(8,128)} async-done(((f32[4096,384]{1,0:T(8,128)}), f32[4096,384]{1,0:T(8,128)}) %all-reduce.5.cloned.1.call-update) | async-done | bytes 6291472 | tf_op jit(solution)/shard_map/psum | solution.py:53
  258.8 0.0 copy-done
  258.8 11.8 %fusion.8 = f32[4096,768]{1,0:T(8,128)} fusion(bf16[384,768]{1,0:T(8,128)(2,1)S(1)} %copy-done, f32[4096,384]{1,0:T(8,128)} %all-reduce.5.cloned.1.call-done), kind=kOutput, calls=%fused_computation.9 | convolution fusion | flops 2430074880 | bytes 19464192 | tf_op jit(solution)/shard_map/dot_general | solution.py:56
  270.6 0.0 copy-start.1
  270.6 0.0 copy-start.4
  270.6 0.0 copy-start.3
  270.6 0.0 reduce-scatter.2.cloned.1.call-update
  270.7 0.3 reduce-window.9
  271.0 0.1 slice.40
  271.7 0.1 slice_reduce_fusion
  271.8 0.1 multiply_bitcast_fusion
  271.9 0.7 select_reduce_fusion
  274.0 0.7 iota_compare_fusion.1
  274.7 1.3 compare_and_fusion
  275.9 167.3 %reduce-scatter.2.cloned.1.call-done = f32[128,768]{1,0:T(8,128)} async-done(((f32[4096,768]{1,0:T(8,128)}), f32[128,768]{1,0:T(8,128)}) %reduce-scatter.2.cloned.1.call-update) | async-done | bytes 393232 | tf_op jit(solution)/shard_map/reduce_scatter | solution.py:55
  443.2 0.0 copy-done.1
  443.2 1.3 convert_reduce_fusion
  444.5 0.0 copy-start.2
  444.5 10.5 %all-reduce.1 = (f32[128,1]{0,1:T(1,128)S(1)}, f32[128,1]{0,1:T(1,128)S(1)}) all-reduce(f32[128,1]{0,1:T(1,128)S(1)} %bitcast.50, f32[128,1]{0,1:T(1,128)S(1)} %bitcast.49), channel_id=1, replica_groups=mesh['cfg'=2,'wide'=32,'narrow'=4] {'narrow'}, use_global_device_ids=true, to_apply=%region_14.15 | all-reduce | flops 256 | bytes 2048 | tf_op jit(solution)/shard_map/psum | solution.py:21
  455.0 0.0 copy-done.4
  455.0 0.3 convolution_multiply_fusion
  455.3 31.1 %psum.47 = f32[128,64]{0,1:T(8,128)S(1)} all-reduce(f32[128,64]{0,1:T(8,128)S(1)} %convolution_multiply_fusion), channel_id=1, replica_groups=mesh['cfg'=2,'wide'=32,'narrow'=4] {'cfg','narrow'}, use_global_device_ids=true, to_apply=%region_15.16 | all-reduce | flops 8192 | bytes 65536 | tf_op jit(solution)/shard_map/psum | solution.py:66
  486.4 0.0 copy-done.3
  486.4 0.6 subtract_select_fusion
  487.1 0.0 copy-done.2
  (5 shorter events, 0.1 us)
Async XLA Ops:
  7.2 251.7 %copy-start = (bf16[384,768]{1,0:T(8,128)(2,1)S(1)}, bf16[384,768]{1,0:T(8,128)(2,1)}, u32[]{:S(2)}) copy-start(bf16[384,768]{1,0:T(8,128)(2,1)} %param.12) | copy-start | bytes 1769476
  7.2 112.9 %all-gather.2.cloned.1.call-start = ((), (), s32[]{:S(2)}) async-start(), calls=%async_computation.1 | async-start | bytes 6488064 | tf_op jit(solution)/shard_map/all_gather | solution.py:49
  25.7 233.1 %all-reduce.5.cloned.1.call-start = ((), (), s32[]{:S(2)}) async-start(), calls=%async_computation.2 | async-start | bytes 12582912 | tf_op jit(solution)/shard_map/psum | solution.py:53
  129.1 314.2 %reduce-scatter.2.cloned.1.call-start = ((), (), s32[]{:S(2)}) async-start(), calls=%async_computation.3 | async-start | bytes 12976128 | tf_op jit(solution)/shard_map/reduce_scatter | solution.py:55
  270.6 172.6 %copy-start.1 = (bf16[1,128,768]{2,1,0:T(8,128)(2,1)S(1)}, bf16[1,128,768]{2,1,0:T(8,128)(2,1)}, u32[]{:S(2)}) copy-start(bf16[1,128,768]{2,1,0:T(8,128)(2,1)} %param.8) | copy-start | bytes 589828
  270.6 184.4 %copy-start.4 = (bf16[768,64]{0,1:T(8,128)(2,1)S(1)}, bf16[768,64]{0,1:T(8,128)(2,1)}, u32[]{:S(2)}) copy-start(bf16[768,64]{0,1:T(8,128)(2,1)} %param.13) | copy-start | bytes 294916
  270.6 215.8 %copy-start.3 = (f32[128,64]{0,1:T(8,128)S(1)}, f32[128,64]{0,1:T(8,128)}, u32[]{:S(2)}) copy-start(f32[128,64]{0,1:T(8,128)} %param.14) | copy-start | bytes 98308
  444.5 42.6 %copy-start.2 = (bf16[128,768]{1,0:T(8,128)(2,1)}, bf16[128,768]{1,0:T(8,128)(2,1)S(1)}, u32[]{:S(2)}) copy-start(bf16[128,768]{1,0:T(8,128)(2,1)S(1)} %get-tuple-element.18) | copy-start | bytes 589828
Sparse Core Ops, SparseCore 0:
  25.8 94.2 all-gather.1
  129.2 129.5 all-reduce.4
  270.8 172.3 reduce-scatter.1
where the time goes:
time: 494 us
  waiting for transfers between devices  391 us (79%)
  blocking collectives  52.4 us (11%)
  matrix products  21.1 us (4%)
  between operations  15.9 us (3%)
  other arithmetic  12.5 us (3%)
    reduce_scatter x1, waiting for transfers between devices, on_device(): lax.psum_scatter(jnp.dot(activated, contract_weight, preferred_element_ty...  167 us
    psum x1, waiting for transfers between devices, on_device(): hidden_pre = lax.psum(hidden_part, 'narrow')  130 us
    all_gather x1, waiting for transfers between devices, on_device(): lax.all_gather(normed, 'wide', axis=0, tiled=True)  94.3 us
    psum x1, blocking collectives, on_device(): guided = lax.psum(velocity_part * copy_weight, ('cfg', 'narrow'))  31.1 us
    psum x2, blocking collectives, feature_norm(): lax.psum((jnp.sum(values, -1, keepdims=True), jnp.sum(values * values, -1...  21.2 us
    dot_general x1, matrix products, on_device(): jnp.dot(activated, contract_weight, preferred_element_type=jnp.float32)  11.8 us
  transfers between devices with their start and end apart: 3, of which 3 were waited for; matrix products, arithmetic and copies ran while one was open for 1% of the time, Pallas kernels for 0%

commit v1 on v0

--- a/solution.py
+++ b/solution.py
@@ -2,6 +2,7 @@
 import jax.numpy as jnp
 from jax import lax
 from jax.sharding import PartitionSpec as P
+from jax.lax import all_gather
 
 D = 3072
 TEXT = 226
@@ -50,7 +51,7 @@
         expand_weight,
         preferred_element_type=jnp.float32,
     )
-    hidden_pre = lax.psum(hidden_part, "narrow")
+    hidden_pre = jnp.sum(all_gather(hidden_part, "narrow"), axis=0)
     activated = jax.nn.gelu(hidden_pre, approximate=True).astype(jnp.bfloat16)
     ff_result = lax.psum_scatter(
         jnp.dot(activated, contract_weight, preferred_element_type=jnp.float32),

time: 494 us -> 602 us (1.22)
  waiting for transfers between devices: 391 us -> 487 us
  other arithmetic: 12.5 us -> 25.3 us
    all_gather x0 -> x1, waiting for transfers between devices: none -> 224 us  [on_device(): hidden_pre = jnp.sum(all_gather(hidden_part, 'narrow'), axis=0)]
    psum x1 -> x0, waiting for transfers between devices: 130 us -> none  [on_device(): hidden_pre = lax.psum(hidden_part, 'narrow')]
    reduce_sum x0 -> x1, other arithmetic: none -> 12.5 us  [on_device(): hidden_pre = jnp.sum(all_gather(hidden_part, 'narrow'), axis=0)]
where the time goes in v1:
time: 602 us
  waiting for transfers between devices  487 us (81%)
  blocking collectives  52.4 us (9%)
  other arithmetic  25.3 us (4%)
  matrix products  21.1 us (4%)
  between operations  15.9 us (3%)
    all_gather x1, waiting for transfers between devices, on_device(): hidden_pre = jnp.sum(all_gather(hidden_part, 'narrow'), axis=0)  224 us
    reduce_scatter x1, waiting for transfers between devices, on_device(): lax.psum_scatter(jnp.dot(activated, contract_weight, preferred_element_ty...  168 us
    all_gather x1, waiting for transfers between devices, on_device(): lax.all_gather(normed, 'wide', axis=0, tiled=True)  94.3 us
    psum x1, blocking collectives, on_device(): guided = lax.psum(velocity_part * copy_weight, ('cfg', 'narrow'))  31.2 us
    psum x2, blocking collectives, feature_norm(): lax.psum((jnp.sum(values, -1, keepdims=True), jnp.sum(values * values, -1...  21.2 us
    reduce_sum x1, other arithmetic, on_device(): hidden_pre = jnp.sum(all_gather(hidden_part, 'narrow'), axis=0)  12.5 us
  transfers between devices with their start and end apart: 3, of which 3 were waited for; matrix products, arithmetic and copies ran while one was open for 1% of the time, Pallas kernels for 0%

profile of v1, /device:TPU:2, one launch (start us, length us, event | category | flops | bytes accessed | tf_op | source)
XLA Modules:
  0.0 601.7 jit_solution(1549023992851632403)
XLA Ops:
  7.2 0.0 copy-start
  7.2 0.0 all-gather.4.cloned.1.call-start
  7.2 1.1 convert_reduce_fusion.1
  8.3 1.1 fusion.21
  9.4 1.1 add_reduce_fusion
  10.5 1.4 fusion.34
  11.9 1.3 compare_and_fusion.1
  13.2 10.7 %all-reduce.2 = (f32[128,1]{0,1:T(1,128)S(1)}, f32[128,1]{0,1:T(1,128)S(1)}) all-reduce(f32[128,1]{0,1:T(1,128)S(1)} %bitcast.50, f32[128,1]{0,1:T(1,128)S(1)} %bitcast.49), channel_id=1, replica_groups=mesh['cfg'=2,'wide'=32,'narrow'=4] {'narrow'}, use_global_device_ids=true, to_apply=%region_5.6 | all-reduce | flops 256 | bytes 2048 | tf_op jit(solution)/shard_map/psum | solution.py:22
  24.0 1.8 fusion.20
  25.8 0.0 all-gather.4.cloned.1.call-update
  25.8 0.0 all-gather.6.cloned.1.call-start
  25.9 94.3 %all-gather.4.cloned.1.call-done = bf16[4096,768]{1,0:T(8,128)(2,1)} async-done(((bf16[128,768]{1,0:T(8,128)(2,1)}), bf16[4096,768]{1,0:T(8,128)(2,1)}) %all-gather.4.cloned.1.call-update) | async-done | bytes 6291472 | tf_op jit(solution)/shard_map/all_gather | solution.py:50
  120.2 9.0 %fusion.41 = f32[4096,384]{1,0:T(8,128)} fusion(bf16[4096,768]{1,0:T(8,128)(2,1)} %all-gather.4.cloned.1.call-done, bf16[768,384]{1,0:T(8,128)(2,1)} %param.11), kind=kOutput, calls=%fused_computation.70 | convolution fusion | flops 2415919104 | bytes 13172736 | tf_op jit(solution)/shard_map/dot_general | solution.py:49
  129.2 0.0 all-gather.6.cloned.1.call-update
  129.2 0.0 reduce-scatter.2.cloned.1.call-start
  129.3 224.0 %all-gather.6.cloned.1.call-done = f32[16384,384]{1,0:T(8,128)} async-done(((f32[4096,384]{1,0:T(8,128)}), f32[16384,384]{1,0:T(8,128)}) %all-gather.6.cloned.1.call-update) | async-done | bytes 25165840 | tf_op jit(solution)/shard_map/all_gather | solution.py:54
  353.3 12.5 %reduce_sum.76 = f32[4096,384]{1,0:T(8,128)} reduce(f32[4,4096,384]{2,1,0:T(8,128)} %bitcast.47, f32[]{:T(128)} %constant.21.clone.1), dimensions={0}, to_apply=%region_6.7 | reduce | flops 4718592 | bytes 31457284 | tf_op jit(solution)/shard_map/reduce_sum | solution.py:54
  365.9 0.0 copy-done
  365.9 11.8 %fusion.8 = f32[4096,768]{1,0:T(8,128)} fusion(bf16[384,768]{1,0:T(8,128)(2,1)S(1)} %copy-done, f32[4096,384]{1,0:T(8,128)} %reduce_sum.76), kind=kOutput, calls=%fused_computation.9 | convolution fusion | flops 2430074880 | bytes 19464192 | tf_op jit(solution)/shard_map/dot_general | solution.py:57
  377.7 0.0 copy-start.1
  377.7 0.0 copy-start.4
  377.7 0.0 copy-start.3
  377.7 0.0 reduce-scatter.2.cloned.1.call-update
  377.7 0.3 reduce-window.9
  378.0 0.1 slice.40
  378.8 0.1 slice_reduce_fusion
  378.9 0.1 multiply_bitcast_fusion
  378.9 0.7 select_reduce_fusion
  381.0 0.7 iota_compare_fusion.1
  381.7 1.3 compare_and_fusion
  383.1 168.3 %reduce-scatter.2.cloned.1.call-done = f32[128,768]{1,0:T(8,128)} async-done(((f32[4096,768]{1,0:T(8,128)}), f32[128,768]{1,0:T(8,128)}) %reduce-scatter.2.cloned.1.call-update) | async-done | bytes 393232 | tf_op jit(solution)/shard_map/reduce_scatter | solution.py:56
  551.4 0.0 copy-done.1
  551.4 1.3 convert_reduce_fusion
  552.6 0.0 copy-start.2
  552.6 10.4 %all-reduce.1 = (f32[128,1]{0,1:T(1,128)S(1)}, f32[128,1]{0,1:T(1,128)S(1)}) all-reduce(f32[128,1]{0,1:T(1,128)S(1)} %bitcast.52, f32[128,1]{0,1:T(1,128)S(1)} %bitcast.51), channel_id=1, replica_groups=mesh['cfg'=2,'wide'=32,'narrow'=4] {'narrow'}, use_global_device_ids=true, to_apply=%region_14.15 | all-reduce | flops 256 | bytes 2048 | tf_op jit(solution)/shard_map/psum | solution.py:22
  563.1 0.0 copy-done.4
  563.1 0.3 convolution_multiply_fusion
  563.4 31.2 %psum.39 = f32[128,64]{0,1:T(8,128)S(1)} all-reduce(f32[128,64]{0,1:T(8,128)S(1)} %convolution_multiply_fusion), channel_id=1, replica_groups=mesh['cfg'=2,'wide'=32,'narrow'=4] {'cfg','narrow'}, use_global_device_ids=true, to_apply=%region_15.16 | all-reduce | flops 8192 | bytes 65536 | tf_op jit(solution)/shard_map/psum | solution.py:67
  594.5 0.0 copy-done.3
  594.6 0.6 subtract_select_fusion
  595.2 0.0 copy-done.2
  (5 shorter events, 0.1 us)
Async XLA Ops:
  7.2 358.7 %copy-start = (bf16[384,768]{1,0:T(8,128)(2,1)S(1)}, bf16[384,768]{1,0:T(8,128)(2,1)}, u32[]{:S(2)}) copy-start(bf16[384,768]{1,0:T(8,128)(2,1)} %param.12) | copy-start | bytes 1769476
  7.2 113.0 %all-gather.4.cloned.1.call-start = ((), (), s32[]{:S(2)}) async-start(), calls=%async_computation.1 | async-start | bytes 6488064 | tf_op jit(solution)/shard_map/all_gather | solution.py:50
  25.8 327.5 %all-gather.6.cloned.1.call-start = ((), (), s32[]{:S(2)}) async-start(), calls=%async_computation.3 | async-start | bytes 31457280 | tf_op jit(solution)/shard_map/all_gather | solution.py:54
  129.2 422.1 %reduce-scatter.2.cloned.1.call-start = ((), (), s32[]{:S(2)}) async-start(), calls=%async_computation.2 | async-start | bytes 12976128 | tf_op jit(solution)/shard_map/reduce_scatter | solution.py:56
  377.7 173.7 %copy-start.1 = (bf16[1,128,768]{2,1,0:T(8,128)(2,1)S(1)}, bf16[1,128,768]{2,1,0:T(8,128)(2,1)}, u32[]{:S(2)}) copy-start(bf16[1,128,768]{2,1,0:T(8,128)(2,1)} %param.8) | copy-start | bytes 589828
  377.7 185.4 %copy-start.4 = (bf16[768,64]{0,1:T(8,128)(2,1)S(1)}, bf16[768,64]{0,1:T(8,128)(2,1)}, u32[]{:S(2)}) copy-start(bf16[768,64]{0,1:T(8,128)(2,1)} %param.13) | copy-start | bytes 294916
  377.7 216.9 %copy-start.3 = (f32[128,64]{0,1:T(8,128)S(1)}, f32[128,64]{0,1:T(8,128)}, u32[]{:S(2)}) copy-start(f32[128,64]{0,1:T(8,128)} %param.14) | copy-start | bytes 98308
  552.6 42.6 %copy-start.2 = (bf16[128,768]{1,0:T(8,128)(2,1)}, bf16[128,768]{1,0:T(8,128)(2,1)S(1)}, u32[]{:S(2)}) copy-start(bf16[128,768]{1,0:T(8,128)(2,1)S(1)} %get-tuple-element.18) | copy-start | bytes 589828
Sparse Core Ops, SparseCore 0:
  25.9 94.2 all-gather.3
  129.4 223.9 all-gather.5
  377.8 173.4 reduce-scatter.1
